TPU v7x, 256 devices: a whole 4x4x8 slice. The times are simulated.
256 devices in a mesh: dp: 8 (over z_lo, y), seq: 32 (over x, z_hi, core).
Axes of the slice: x: 4, y: 4, z: 8 (z_hi: 4, z_lo: 2; z = z_hi * 2 + z_lo), core: 2. Of those that a mesh axis runs over, the one named last changes fastest.
Arguments:
- tokens: bfloat16 [8, 8192, 4096], P('dp', 'seq'), may hold values from -6 to 6
- queries: bfloat16 [8, 8192, 128], P('dp', 'seq'), may hold values from -6 to 6
- key_vectors: bfloat16 [8, 8192, 128], P('dp', 'seq'), may hold values from -6 to 6
- doc_position: int32 [8, 8192], P('dp', 'seq'), may hold values from 0 to 8191, as said below
- value_scores: float32 [8, 8192, 4], P('dp', 'seq'), may hold values from 0.1 to 1
- value_experts: int32 [8, 8192, 2], P('dp', 'seq'), may hold values from 0 to 3, all different within a row
- output_scores: float32 [8, 8192, 4], P('dp', 'seq'), may hold values from 0.1 to 1
- output_experts: int32 [8, 8192, 2], P('dp', 'seq'), may hold values from 0 to 3, all different within a row
- value_panels: bfloat16 [4096, 512], P('seq'), may hold values from -0.09375 to 0.09375
- output_panels: bfloat16 [4096, 512], P('seq'), may hold values from -3 to 3
- cotangent: bfloat16 [8, 8192, 4096], P('dp', 'seq'), may hold values from -0.625 to 0.625
Outputs:
- layer_output: bfloat16 [8, 8192, 4096], P('dp', 'seq')
- grad_tokens: bfloat16 [8, 8192, 4096], P('dp', 'seq')
- grad_queries: bfloat16 [8, 8192, 128], P('dp', 'seq')
- grad_keys: bfloat16 [8, 8192, 128], P('dp', 'seq')
- grad_value: float32 [4096, 512], P('seq')
- grad_output: float32 [4096, 512], P('seq')
Inputs may be any that keep to these rules, and one draw needn't show every extreme that they name: doc_position[b, i] is i minus the first position of the document that holds position i; position 0 starts a document in every sequence; sequence 0 is one document; every other sequence holds one to four documents.
All inputs are finite; a program needn't handle non-finite values.
Results may differ from a plain program's by a relative error of at most 0.035.
Values may be sent and summed in bfloat16 or wider, within the bound.
No kernel may reach another device: no remote copies, remote signals or barrier semaphores. Data moves between devices by JAX's collectives and lax.ppermute only.
A program may use at most 128 MiB of HBM per device.

v0:
```python
import jax
import jax.numpy as jnp
from jax import lax
from jax.sharding import PartitionSpec as P


def expert_gates(scores, chosen, experts):
    chosen_hit = chosen[:, :, None] == lax.iota(jnp.int32, experts)[None, None, :]
    return jnp.where(jnp.any(chosen_hit, axis=1), scores, jnp.float32(0.0))


def contract_last(left, right):
    return lax.dot_general(
        left, right, (((1,), (1,)), ((), ())), preferred_element_type=jnp.float32
    )


def contract_first(left, right):
    return lax.dot_general(
        left, right, (((0,), (0,)), ((), ())), preferred_element_type=jnp.float32
    )


def body(
    tokens,
    queries,
    key_vectors,
    doc_position,
    value_scores,
    value_experts,
    output_scores,
    output_experts,
    value_panels,
    output_panels,
    cotangent,
):
    tok_block = tokens[0]
    query_block = queries[0]
    own_keys = key_vectors[0]
    positions = doc_position[0]
    grad_rows = cotangent[0]
    tok_rows = tok_block.shape[0]
    head_size = query_block.shape[1]
    experts = value_scores.shape[2]
    panel_width = value_panels.shape[1]
    value_gate = expert_gates(value_scores[0], value_experts[0], experts)
    output_gate = expert_gates(output_scores[0], output_experts[0], experts)
    value_full, output_full = (
        lax.all_gather(value_panels, "seq", axis=0, tiled=True),
        lax.all_gather(output_panels, "seq", axis=0, tiled=True),
    )
    projection = jnp.dot(tok_block, value_full, preferred_element_type=jnp.float32)
    value_vec = jnp.sum(
        projection.reshape(tok_rows, experts, head_size) * value_gate[:, :, None], axis=1
    ).astype(jnp.bfloat16)
    keys_all, values_all = (
        lax.all_gather(own_keys, "seq", axis=0, tiled=True),
        lax.all_gather(value_vec, "seq", axis=0, tiled=True),
    )
    length = keys_all.shape[0]
    score_scale = head_size ** (-0.5)
    query_index = lax.axis_index("seq") * tok_rows + lax.iota(jnp.int32, tok_rows)
    key_index = lax.iota(jnp.int32, length)
    visible = (key_index[None, :] <= query_index[:, None]) & (
        query_index[:, None] - key_index[None, :] <= positions[:, None]
    )
    masked = jnp.where(visible, contract_last(query_block, keys_all) * score_scale, -jnp.inf)
    row_max = jnp.max(masked, axis=1)
    log_total = row_max + jnp.log(jnp.sum(jnp.exp(masked - row_max[:, None]), axis=1))
    attn_prob = jnp.exp(masked - log_total[:, None])
    prob_low = attn_prob.astype(jnp.bfloat16)
    attended = jnp.dot(prob_low, values_all, preferred_element_type=jnp.float32).astype(
        jnp.bfloat16
    )
    expanded = (
        (output_gate[:, :, None] * attended.astype(jnp.float32)[:, None, :])
        .reshape(tok_rows, panel_width)
        .astype(jnp.bfloat16)
    )
    layer_output = contract_last(expanded, output_full).astype(jnp.bfloat16)
    pulled = jnp.dot(grad_rows, output_full, preferred_element_type=jnp.float32)
    dattended = jnp.sum(
        pulled.reshape(tok_rows, experts, head_size) * output_gate[:, :, None], axis=1
    ).astype(jnp.bfloat16)
    row_delta = jnp.sum(dattended.astype(jnp.float32) * attended.astype(jnp.float32), axis=1)
    dweights = contract_last(dattended, values_all)
    dscores = (attn_prob * (dweights - row_delta[:, None])).astype(jnp.bfloat16)
    grad_queries = (
        jnp.dot(dscores, keys_all, preferred_element_type=jnp.float32) * score_scale
    ).astype(jnp.bfloat16)
    key_term = contract_first(dscores, query_block) * score_scale
    value_term = contract_first(prob_low, dattended)
    dkey_sum, dvalue_sum = (
        lax.psum_scatter(
            key_term.astype(jnp.bfloat16), "seq", scatter_dimension=0, tiled=True
        ).astype(jnp.float32),
        lax.psum_scatter(
            value_term.astype(jnp.bfloat16), "seq", scatter_dimension=0, tiled=True
        ).astype(jnp.float32),
    )
    grad_keys = dkey_sum.astype(jnp.bfloat16)
    dvalue = dvalue_sum.astype(jnp.bfloat16)
    value_grad = (
        (value_gate[:, :, None] * dvalue.astype(jnp.float32)[:, None, :])
        .reshape(tok_rows, panel_width)
        .astype(jnp.bfloat16)
    )
    grad_tokens = contract_last(value_grad, value_full).astype(jnp.bfloat16)
    term_value = contract_first(tok_block, value_grad)
    term_output = contract_first(grad_rows, expanded)
    owned = lax.psum_scatter(
        jnp.concatenate([term_value, term_output], axis=1).astype(jnp.bfloat16),
        "seq",
        scatter_dimension=0,
        tiled=True,
    )
    summed = lax.psum(owned, "dp").astype(jnp.float32)
    return (
        layer_output[None],
        grad_tokens[None],
        grad_queries[None],
        grad_keys[None],
        summed[:, :panel_width],
        summed[:, panel_width:],
    )


def solution(mesh):
    in_specs = (
        P("dp", "seq", None),
        P("dp", "seq", None),
        P("dp", "seq", None),
        P("dp", "seq"),
        P("dp", "seq", None),
        P("dp", "seq", None),
        P("dp", "seq", None),
        P("dp", "seq", None),
        P("seq", None),
        P("seq", None),
        P("dp", "seq", None),
    )
    out_specs = (
        P("dp", "seq", None),
        P("dp", "seq", None),
        P("dp", "seq", None),
        P("dp", "seq", None),
        P("seq", None),
        P("seq", None),
    )
    return jax.shard_map(body, mesh=mesh, in_specs=in_specs, out_specs=out_specs, check_vma=False)
```

profile of v0, /device:TPU:8, one launch (start us, length us, event | category | flops | bytes accessed | tf_op | source)
XLA Modules:
  0.0 667.2 jit_solution(10940611194924719588)
XLA Ops:
  10.9 57.3 %all-gather.12.cloned.1.call-done = bf16[1,8192,128]{2,1,0:T(8,128)(2,1)} async-done(((bf16[1,256,128]{2,1,0:T(8,128)(2,1)}), bf16[1,8192,128]{2,1,0:T(8,128)(2,1)}) %all-gather.12.cloned.1.call-update) | async-done | bytes 2097168 | tf_op jit(solution)/shard_map/all_gather | solution.py:57
  68.2 4.6 fusion.50
  74.1 1.9 copy-done.2
  76.0 52.1 %all-gather.10.cloned.1.call-done = bf16[4096,512]{1,0:T(8,128)(2,1)} async-done(((bf16[128,512]{1,0:T(8,128)(2,1)}), bf16[4096,512]{1,0:T(8,128)(2,1)}) %all-gather.10.cloned.1.call-update) | async-done | bytes 4194320 | tf_op jit(solution)/shard_map/all_gather | solution.py:50
  128.1 6.4 copy.46
  134.5 4.1 fusion.25
  138.7 6.7 convolution_convert_fusion
  145.5 43.1 %all-gather.6.cloned.1.call-done = bf16[4096,512]{1,0:T(8,128)(2,1)} async-done(((bf16[128,512]{1,0:T(8,128)(2,1)}), bf16[4096,512]{1,0:T(8,128)(2,1)}) %all-gather.6.cloned.1.call-update) | async-done | bytes 4194320 | tf_op jit(solution)/shard_map/all_gather | solution.py:49
  188.6 6.4 copy.43
  195.0 4.1 fusion.28
  199.4 82.5 %reduce-scatter.6.cloned.1.call-done = bf16[256,128]{1,0:T(8,128)(2,1)} async-done(((bf16[8192,128]{1,0:T(8,128)(2,1)}), bf16[256,128]{1,0:T(8,128)(2,1)}) %reduce-scatter.6.cloned.1.call-update) | async-done | bytes 65552 | tf_op jit(solution)/shard_map/reduce_scatter | solution.py:97
  283.1 3.2 fusion.6
  286.3 50.8 %all-gather.8.cloned.1.call-done = bf16[8192,128]{1,0:T(8,128)(2,1)} async-done(((bf16[256,128]{1,0:T(8,128)(2,1)}), bf16[8192,128]{1,0:T(8,128)(2,1)}) %all-gather.8.cloned.1.call-update) | async-done | bytes 2097168 | tf_op jit(solution)/shard_map/all_gather | solution.py:58
  337.1 5.7 multiply_reduce_fusion
  343.3 3.2 fusion.7
  346.5 7.8 %pad_maximum_fusion = bf16[4096,1024]{0,1:T(8,128)(2,1)} fusion(bf16[4096,512]{0,1:T(8,128)(2,1)} %fusion.7, bf16[4096,512]{0,1:T(8,128)(2,1)} %fusion.6), kind=kLoop, calls=%fused_computation.8 | loop fusion | flops 16777216 | bytes 16777216 | tf_op jit(solution)/shard_map/concatenate | solution.py:112
  354.3 12.0 %copy.51 = bf16[4096,1024]{1,0:T(8,128)(2,1)} copy(bf16[4096,1024]{0,1:T(8,128)(2,1)} %pad_maximum_fusion) | data formatting | bytes 16777216
  367.9 6.1 fusion.2
  374.0 111.0 %reduce-scatter.10.cloned.1.call-done = bf16[128,1024]{1,0:T(8,128)(2,1)} async-done(((bf16[4096,1024]{1,0:T(8,128)(2,1)}), bf16[128,1024]{1,0:T(8,128)(2,1)}) %reduce-scatter.10.cloned.1.call-update) | async-done | bytes 262160
  487.0 4.8 fusion.3
  491.9 5.0 fusion.9
  496.9 2.6 fusion.8
  502.4 60.6 %all-reduce.2.cloned.1.call-done = bf16[128,1024]{0,1:T(8,128)(2,1)} async-done(((bf16[128,1024]{0,1:T(8,128)(2,1)}), bf16[128,1024]{0,1:T(8,128)(2,1)}) %all-reduce.2.cloned.1.call-update) | async-done | bytes 262160 | tf_op jit(solution)/shard_map/psum | solution.py:117
  565.7 94.6 %reduce-scatter.8.cloned.1.call-done = bf16[256,128]{1,0:T(8,128)(2,1)} async-done(((bf16[8192,128]{1,0:T(8,128)(2,1)}), bf16[256,128]{1,0:T(8,128)(2,1)}) %reduce-scatter.8.cloned.1.call-update) | async-done | bytes 65552 | tf_op jit(solution)/shard_map/reduce_scatter | solution.py:94
  (56 shorter events, 16.3 us)
Async XLA Ops:
  7.2 187.8 %copy-start = (bf16[1,256,4096]{2,1,0:T(8,128)(2,1)S(1)}, bf16[1,256,4096]{2,1,0:T(8,128)(2,1)}, u32[]{:S(2)}) copy-start(bf16[1,256,4096]{2,1,0:T(8,128)(2,1)} %param.11) | copy-start | bytes 6291460
  7.2 61.0 %all-gather.12.cloned.1.call-start = ((), (), s32[]{:S(2)}) async-start(), calls=%async_computation.9 | async-start | bytes 2162688 | tf_op jit(solution)/shard_map/all_gather | solution.py:57
  7.9 120.2 %all-gather.10.cloned.1.call-start = ((), (), s32[]{:S(2)}) async-start(), calls=%async_computation.5 | async-start | bytes 4325376 | tf_op jit(solution)/shard_map/all_gather | solution.py:50
  8.7 179.9 %all-gather.6.cloned.1.call-start = ((), (), s32[]{:S(2)}) async-start(), calls=%async_computation.3 | async-start | bytes 4325376 | tf_op jit(solution)/shard_map/all_gather | solution.py:49
  9.4 272.5 %reduce-scatter.6.cloned.1.call-start = ((), (), s32[]{:S(2)}) async-start(), calls=%async_computation.6 | async-start | bytes 2162688 | tf_op jit(solution)/shard_map/reduce_scatter | solution.py:97
  72.8 3.2 copy-start.2
  138.7 6.8 %copy-start.10 = (s32[1,256,2]{1,2,0:T(2,128)S(1)}, s32[1,256,2]{1,2,0:T(2,128)}, u32[]{:S(2)}) copy-start(s32[1,256,2]{1,2,0:T(2,128)} %param.16) | copy-start | bytes 6148
  138.7 6.8 %copy-start.9 = (f32[1,256,4]{1,2,0:T(4,128)S(1)}, f32[1,256,4]{1,2,0:T(4,128)}, u32[]{:S(2)}) copy-start(f32[1,256,4]{1,2,0:T(4,128)} %param.15) | copy-start | bytes 12292
  145.4 191.7 %all-gather.8.cloned.1.call-start = ((), (), s32[]{:S(2)}) async-start(), calls=%async_computation.4 | async-start | bytes 2162688 | tf_op jit(solution)/shard_map/all_gather | solution.py:58
  199.1 285.8 %reduce-scatter.10.cloned.1.call-start = ((), (), s32[]{:S(2)}) async-start(), calls=%async_computation.10 | async-start | bytes 8650752
  286.3 57.0 %copy-start.6 = (bf16[1,256,4096]{2,1,0:T(8,128)(2,1)S(1)}, bf16[1,256,4096]{2,1,0:T(8,128)(2,1)}, u32[]{:S(2)}) copy-start(bf16[1,256,4096]{2,1,0:T(8,128)(2,1)} %param.21) | copy-start | bytes 6291460
  366.3 1.6 copy-start.5
  366.3 196.7 %all-reduce.2.cloned.1.call-start = ((), (), s32[]{:S(2)}) async-start(), calls=%async_computation.8 | async-start | bytes 524288 | tf_op jit(solution)/shard_map/psum | solution.py:117
  367.9 119.1 %copy-start.8 = (bf16[1,256,128]{2,1,0:T(8,128)(2,1)S(1)}, bf16[1,256,128]{2,1,0:T(8,128)(2,1)}, u32[]{:S(2)}) copy-start(bf16[1,256,128]{2,1,0:T(8,128)(2,1)} %param.12) | copy-start | bytes 196612
  486.7 173.6 %reduce-scatter.8.cloned.1.call-start = ((), (), s32[]{:S(2)}) async-start(), calls=%async_computation.7 | async-start | bytes 2162688 | tf_op jit(solution)/shard_map/reduce_scatter | solution.py:94
  491.9 5.0 copy-start.4
  496.9 2.6 copy-start.3
  496.9 3.6 copy-start.7
  496.9 163.5 %copy-start.1 = (bf16[1,256,4096]{2,1,0:T(8,128)(2,1)S(1)}, bf16[1,256,4096]{2,1,0:T(8,128)(2,1)}, u32[]{:S(2)}) copy-start(bf16[1,256,4096]{2,1,0:T(8,128)(2,1)} %param.11) | copy-start | bytes 6291460
Sparse Core Ops, SparseCore 0:
  10.6 57.5 all-gather.11
  70.7 57.3 all-gather.9
  130.6 57.8 all-gather.5
  192.8 88.9 reduce-scatter.5
  284.8 52.2 all-gather.7
  366.5 118.4 reduce-scatter.9
  488.3 74.6 all-reduce.1
  567.4 92.8 reduce-scatter.7
where the time goes:
time: 668 us; the launch traced here: 667 us
  waiting for transfers between devices  554 us (83%)
  matrix products  52 us (8%)
  local copies, waits for them, and re-layouts  34.1 us (5%)
  between operations  14.3 us (2%)
  other arithmetic  11.8 us (2%)
    unnamed x9, waiting for transfers between devices  113 us
    reduce_scatter x1, waiting for transfers between devices, body(): lax.psum_scatter(key_term.astype(jnp.bfloat16), 'seq', scatter_dimension=...  94.6 us
    reduce_scatter x1, waiting for transfers between devices, body(): lax.psum_scatter(value_term.astype(jnp.bfloat16), 'seq', scatter_dimensio...  82.5 us
    psum x1, waiting for transfers between devices, body(): summed = lax.psum(owned, 'dp').astype(jnp.float32)  60.6 us
    all_gather x1, waiting for transfers between devices, body(): lax.all_gather(own_keys, 'seq', axis=0, tiled=True)  57.3 us
    all_gather x1, waiting for transfers between devices, body(): lax.all_gather(output_panels, 'seq', axis=0, tiled=True)  52.1 us
    all_gather x1, waiting for transfers between devices, body(): lax.all_gather(value_vec, 'seq', axis=0, tiled=True)  50.8 us
    all_gather x1, waiting for transfers between devices, body(): lax.all_gather(value_panels, 'seq', axis=0, tiled=True)  43.1 us
  transfers between devices with their start and end apart: 8, of which 8 were waited for; matrix products, arithmetic and copies ran while one was open for 9% of the time, Pallas kernels for 0%

commit v1 on v0

--- a/solution.py
+++ b/solution.py
@@ -54,7 +54,9 @@
         projection.reshape(tok_rows, experts, head_size) * value_gate[:, :, None], axis=1
     ).astype(jnp.bfloat16)
     keys_all, values_all = (
-        lax.all_gather(own_keys, "seq", axis=0, tiled=True),
+        jnp.concatenate(
+            lax.all_to_all(jnp.stack([own_keys] * lax.axis_size("seq")), "seq", 0, 0), axis=0
+        ),
         lax.all_gather(value_vec, "seq", axis=0, tiled=True),
     )
     length = keys_all.shape[0]

time: 668 us -> 637 us (0.954)
  waiting for transfers between devices: 554 us -> 509 us
  starting transfers between devices: 0.72 us -> 12.1 us
    all_to_all x0 -> x1, waiting for transfers between devices: none -> 59.9 us  [body(): lax.all_to_all(jnp.stack([own_keys] * lax.axis_size('seq')), 'seq', 0, 0)]
    all_gather x1 -> x0, waiting for transfers between devices: 57.3 us -> none  [body(): lax.all_gather(own_keys, 'seq', axis=0, tiled=True)]
    all_gather x1, waiting for transfers between devices: 52.1 us -> 4.09 us  [body(): lax.all_gather(output_panels, 'seq', axis=0, tiled=True)]
    all_to_all x0 -> x1, starting transfers between devices: none -> 11.4 us  [body(): lax.all_to_all(jnp.stack([own_keys] * lax.axis_size('seq')), 'seq', 0, 0)]
    unnamed x26 -> x30, local copies, waits for them, and re-layouts: 19.9 us -> 18.9 us
    unnamed x9 -> x8, waiting for transfers between devices: 113 us -> 112 us
  transfers between devices with their start and end apart: 8 -> 8, of which waited for: 8 -> 8; matrix products, arithmetic and copies ran while one was open for 9% -> 10% of each run, Pallas kernels for 0% -> 0%
where the time goes in v1:
time: 637 us; the launch traced here: 636 us
  waiting for transfers between devices  509 us (80%)
  matrix products  53.5 us (8%)
  local copies, waits for them, and re-layouts  35.8 us (6%)
  between operations  14.4 us (2%)
  starting transfers between devices  12.1 us (2%)
  other arithmetic  10.5 us (2%)
    unnamed x8, waiting for transfers between devices  112 us
    reduce_scatter x1, waiting for transfers between devices, body(): lax.psum_scatter(key_term.astype(jnp.bfloat16), 'seq', scatter_dimension=...  94.6 us
    reduce_scatter x1, waiting for transfers between devices, body(): lax.psum_scatter(value_term.astype(jnp.bfloat16), 'seq', scatter_dimensio...  82.6 us
    all_to_all x1, waiting for transfers between devices, body(): lax.all_to_all(jnp.stack([own_keys] * lax.axis_size('seq')), 'seq', 0, 0)  59.9 us
    psum x1, waiting for transfers between devices, body(): summed = lax.psum(owned, 'dp').astype(jnp.float32)  59.6 us
    all_gather x1, waiting for transfers between devices, body(): lax.all_gather(value_vec, 'seq', axis=0, tiled=True)  50.9 us
    all_gather x1, waiting for transfers between devices, body(): lax.all_gather(value_panels, 'seq', axis=0, tiled=True)  45 us
    unnamed x30, local copies, waits for them, and re-layouts  18.9 us
  transfers between devices with their start and end apart: 8, of which 8 were waited for; matrix products, arithmetic and copies ran while one was open for 10% of the time, Pallas kernels for 0%

profile of v1, /device:TPU:8, one launch (start us, length us, event | category | flops | bytes accessed | tf_op | source)
XLA Modules:
  0.0 635.5 jit_solution(11670705400393437149)
XLA Ops:
  11.3 11.4 %all-to-all-start = ((bf16[32,256,128]{2,1,0:T(8,128)(2,1)}), bf16[32,256,128]{2,1,0:T(8,128)(2,1)}, u32[]{:S(2)}, u32[]{:S(2)}) async-start(bf16[32,256,128]{2,1,0:T(8,128)(2,1)} %stack.3), calls=%async_computation | async-start | bytes 4194304 | tf_op jit(solution)/shard_map/all_to_all | solution.py:58
  22.9 59.9 %all-to-all-done = bf16[32,256,128]{2,1,0:T(8,128)(2,1)} async-done(((bf16[32,256,128]{2,1,0:T(8,128)(2,1)}), bf16[32,256,128]{2,1,0:T(8,128)(2,1)}, u32[]{:S(2)}, u32[]{:S(2)}) %all-to-all-start) | async-done | bytes 2097184 | tf_op jit(solution)/shard_map/all_to_all | solution.py:58
  82.8 4.7 fusion.40
  90.7 4.1 all-gather.8.cloned.1.call-done
  94.8 6.4 %copy.46 = bf16[512,4096]{1,0:T(8,128)(2,1)} copy(bf16[512,4096]{0,1:T(8,128)(2,1)} %bitcast.70) | data formatting | bytes 8388608 | tf_op jit(solution)/shard_map/dot_general | solution.py:83
  101.2 4.1 fusion.22
  105.5 6.5 %convolution_convert_fusion = bf16[8192,128]{1,0:T(8,128)(2,1)} fusion(bf16[256,128]{0,1:T(8,128)(2,1)S(1)} %copy.47, f32[256,8192]{1,0:T(8,128)} %copy-done.2, f32[256]{0:T(256)S(1)} %log_add_fusion), kind=kOutput, calls=%fused_computation.7 | convolution fusion | flops 542113792 | bytes 10552320 | tf_op jit(solution)/shard_map/dot_general | solution.py:19
  112.1 45.0 %all-gather.4.cloned.1.call-done = bf16[4096,512]{1,0:T(8,128)(2,1)} async-done(((bf16[128,512]{1,0:T(8,128)(2,1)}), bf16[4096,512]{1,0:T(8,128)(2,1)}) %all-gather.4.cloned.1.call-update) | async-done | bytes 4194320 | tf_op jit(solution)/shard_map/all_gather | solution.py:49
  157.2 6.4 %copy.43 = bf16[512,4096]{1,0:T(8,128)(2,1)} copy(bf16[512,4096]{0,1:T(8,128)(2,1)} %bitcast.71) | data formatting | bytes 8388608 | tf_op jit(solution)/shard_map/dot_general | solution.py:52
  163.6 4.1 fusion.25
  167.9 82.6 %reduce-scatter.6.cloned.1.call-done = bf16[256,128]{1,0:T(8,128)(2,1)} async-done(((bf16[8192,128]{1,0:T(8,128)(2,1)}), bf16[256,128]{1,0:T(8,128)(2,1)}) %reduce-scatter.6.cloned.1.call-update) | async-done | bytes 65552 | tf_op jit(solution)/shard_map/reduce_scatter | solution.py:99
  251.7 3.2 fusion.6
  254.9 50.9 %all-gather.6.cloned.1.call-done = bf16[8192,128]{1,0:T(8,128)(2,1)} async-done(((bf16[256,128]{1,0:T(8,128)(2,1)}), bf16[8192,128]{1,0:T(8,128)(2,1)}) %all-gather.6.cloned.1.call-update) | async-done | bytes 2097168 | tf_op jit(solution)/shard_map/all_gather | solution.py:60
  305.8 5.7 multiply_reduce_fusion
  312.0 3.2 fusion.7
  315.2 7.8 %pad_maximum_fusion = bf16[4096,1024]{0,1:T(8,128)(2,1)} fusion(bf16[4096,512]{0,1:T(8,128)(2,1)} %fusion.7, bf16[4096,512]{0,1:T(8,128)(2,1)} %fusion.6), kind=kLoop, calls=%fused_computation.8 | loop fusion | flops 16777216 | bytes 16777216 | tf_op jit(solution)/shard_map/concatenate | solution.py:114
  323.0 12.0 %copy.51 = bf16[4096,1024]{1,0:T(8,128)(2,1)} copy(bf16[4096,1024]{0,1:T(8,128)(2,1)} %pad_maximum_fusion) | data formatting | bytes 16777216
  336.6 6.0 fusion.2
  342.6 111.0 %reduce-scatter.10.cloned.1.call-done = bf16[128,1024]{1,0:T(8,128)(2,1)} async-done(((bf16[4096,1024]{1,0:T(8,128)(2,1)}), bf16[128,1024]{1,0:T(8,128)(2,1)}) %reduce-scatter.10.cloned.1.call-update) | async-done | bytes 262160
  455.7 4.8 fusion.3
  460.6 5.0 fusion.9
  468.2 3.5 fusion.30
  471.7 59.6 %all-reduce.2.cloned.1.call-done = bf16[128,1024]{0,1:T(8,128)(2,1)} async-done(((bf16[128,1024]{0,1:T(8,128)(2,1)}), bf16[128,1024]{0,1:T(8,128)(2,1)}) %all-reduce.2.cloned.1.call-update) | async-done | bytes 262160 | tf_op jit(solution)/shard_map/psum | solution.py:119
  534.0 94.6 %reduce-scatter.8.cloned.1.call-done = bf16[256,128]{1,0:T(8,128)(2,1)} async-done(((bf16[8192,128]{1,0:T(8,128)(2,1)}), bf16[256,128]{1,0:T(8,128)(2,1)}) %reduce-scatter.8.cloned.1.call-update) | async-done | bytes 65552 | tf_op jit(solution)/shard_map/reduce_scatter | solution.py:96
  (60 shorter events, 18.5 us)
Async XLA Ops:
  7.2 156.4 %copy-start = (bf16[1,256,4096]{2,1,0:T(8,128)(2,1)S(1)}, bf16[1,256,4096]{2,1,0:T(8,128)(2,1)}, u32[]{:S(2)}) copy-start(bf16[1,256,4096]{2,1,0:T(8,128)(2,1)} %param.11) | copy-start | bytes 6291460
  7.2 15.7 %copy-start.10 = (s32[1,256,2]{1,2,0:T(2,128)S(1)}, s32[1,256,2]{1,2,0:T(2,128)}, u32[]{:S(2)}) copy-start(s32[1,256,2]{1,2,0:T(2,128)} %param.18) | copy-start | bytes 6148
  7.2 15.7 %copy-start.8 = (f32[1,256,4]{1,2,0:T(4,128)S(1)}, f32[1,256,4]{1,2,0:T(4,128)}, u32[]{:S(2)}) copy-start(f32[1,256,4]{1,2,0:T(4,128)} %param.17) | copy-start | bytes 12292
  7.2 75.6 %copy-start.7 = (bf16[1,256,128]{2,1,0:T(8,128)(2,1)S(1)}, bf16[1,256,128]{2,1,0:T(8,128)(2,1)}, u32[]{:S(2)}) copy-start(bf16[1,256,128]{2,1,0:T(8,128)(2,1)} %param.12) | copy-start | bytes 196612
  7.2 75.6 %copy-start.12 = (s32[1,256]{1,0:T(1,128)S(1)}, s32[1,256]{1,0:T(1,128)}, u32[]{:S(2)}) copy-start(s32[1,256]{1,0:T(1,128)} %param.14) | copy-start | bytes 3076
  7.2 87.6 %all-gather.8.cloned.1.call-start = ((), (), s32[]{:S(2)}) async-start(), calls=%async_computation.6 | async-start | bytes 4325376 | tf_op jit(solution)/shard_map/all_gather | solution.py:50
  8.0 149.2 %all-gather.4.cloned.1.call-start = ((), (), s32[]{:S(2)}) async-start(), calls=%async_computation.4 | async-start | bytes 4325376 | tf_op jit(solution)/shard_map/all_gather | solution.py:49
  11.3 71.5 %all-to-all-start = ((bf16[32,256,128]{2,1,0:T(8,128)(2,1)}), bf16[32,256,128]{2,1,0:T(8,128)(2,1)}, u32[]{:S(2)}, u32[]{:S(2)}) async-start(bf16[32,256,128]{2,1,0:T(8,128)(2,1)} %stack.3), calls=%async_computation | async-start | bytes 4194304 | tf_op jit(solution)/shard_map/all_to_all | solution.py:58
  22.8 227.7 %reduce-scatter.6.cloned.1.call-start = ((), (), s32[]{:S(2)}) async-start(), calls=%async_computation.7 | async-start | bytes 2162688 | tf_op jit(solution)/shard_map/reduce_scatter | solution.py:99
  87.5 3.2 copy-start.2
  105.5 6.6 %copy-start.11 = (s32[1,256,2]{1,2,0:T(2,128)S(1)}, s32[1,256,2]{1,2,0:T(2,128)}, u32[]{:S(2)}) copy-start(s32[1,256,2]{1,2,0:T(2,128)} %param.16) | copy-start | bytes 6148
  105.5 6.6 %copy-start.9 = (f32[1,256,4]{1,2,0:T(4,128)S(1)}, f32[1,256,4]{1,2,0:T(4,128)}, u32[]{:S(2)}) copy-start(f32[1,256,4]{1,2,0:T(4,128)} %param.15) | copy-start | bytes 12292
  112.0 193.8 %all-gather.6.cloned.1.call-start = ((), (), s32[]{:S(2)}) async-start(), calls=%async_computation.5 | async-start | bytes 2162688 | tf_op jit(solution)/shard_map/all_gather | solution.py:60
  167.7 285.9 %reduce-scatter.10.cloned.1.call-start = ((), (), s32[]{:S(2)}) async-start(), calls=%async_computation.10 | async-start | bytes 8650752
  254.9 57.1 %copy-start.6 = (bf16[1,256,4096]{2,1,0:T(8,128)(2,1)S(1)}, bf16[1,256,4096]{2,1,0:T(8,128)(2,1)}, u32[]{:S(2)}) copy-start(bf16[1,256,4096]{2,1,0:T(8,128)(2,1)} %param.21) | copy-start | bytes 6291460
  335.0 1.6 copy-start.5
  335.0 196.3 %all-reduce.2.cloned.1.call-start = ((), (), s32[]{:S(2)}) async-start(), calls=%async_computation.9 | async-start | bytes 524288 | tf_op jit(solution)/shard_map/psum | solution.py:119
  455.5 173.2 %reduce-scatter.8.cloned.1.call-start = ((), (), s32[]{:S(2)}) async-start(), calls=%async_computation.8 | async-start | bytes 2162688 | tf_op jit(solution)/shard_map/reduce_scatter | solution.py:96
  460.6 5.0 copy-start.4
  465.6 2.6 copy-start.3
  465.6 163.1 %copy-start.1 = (bf16[1,256,4096]{2,1,0:T(8,128)(2,1)S(1)}, bf16[1,256,4096]{2,1,0:T(8,128)(2,1)}, u32[]{:S(2)}) copy-start(bf16[1,256,4096]{2,1,0:T(8,128)(2,1)} %param.11) | copy-start | bytes 6291460
Sparse Core Ops, SparseCore 0:
  10.6 84.1 all-gather.7
  97.4 59.7 all-gather.3
  161.6 88.8 reduce-scatter.5
  253.5 52.2 all-gather.5
  335.2 118.4 reduce-scatter.9
  456.9 74.4 all-reduce.1
  535.8 92.8 reduce-scatter.7
